TPU v7x, 256 devices: a whole 4x4x8 slice. The times are simulated.
256 devices in a mesh: seq: 32 (over y, x, core), chan: 8 (over z).
Axes of the slice: x: 4, y: 4, z: 8, core: 2. Of those that a mesh axis runs over, the one named last changes fastest.
Arguments:
- conv_in: bfloat16 [32, 512, 512], P(None, 'seq', 'chan'), may hold values from -4 to 4
- conv_gate: bfloat16 [32, 512, 512], P(None, 'seq', 'chan'), may hold values from -4 to 4
- long_filter: float32 [32, 512, 512], P(None, 'seq', 'chan'), may hold values from -1.1 to 1.1
- skip_gain: float32 [512], P('chan'), may hold values from 0.5 to 1.5
- queries: bfloat16 [32, 512, 1024], P(None, 'seq', 'chan'), may hold values from -40 to 40
- keys_in: bfloat16 [32, 512, 1024], P(None, 'seq', 'chan'), may hold values from -40 to 40
- w_value: bfloat16 [512, 1024], P(None, 'chan'), may hold values from -0.25 to 0.25
Outputs:
- conv_out: bfloat16 [32, 512, 512], P(None, 'seq', 'chan')
- attended: bfloat16 [32, 512, 1024], P(None, 'seq', 'chan')
All inputs are finite; a program needn't handle non-finite values.
Results may differ from a plain program's by a relative error of at most 0.015.
Values may be sent and summed in bfloat16 or wider, within the bound.
A program may use at most 64 MiB of HBM per device.

v0:
```python
import math
import jax
import jax.numpy as jnp
from jax import lax
from jax.sharding import PartitionSpec as P


def mixdot(form, left, right):
    return jnp.einsum(form, left, right, precision=lax.Precision.HIGHEST)


def channel_convolve(signal, long_filter):
    moved_sig, moved_tap = (
        lax.all_to_all(
            signal.astype(jnp.bfloat16), "seq", split_axis=2, concat_axis=1, tiled=True
        ).astype(signal.dtype),
        lax.all_to_all(
            long_filter.astype(jnp.bfloat16), "seq", split_axis=2, concat_axis=1, tiled=True
        ).astype(long_filter.dtype),
    )
    blocks = moved_sig.shape[0]
    length_q = moved_sig.shape[1]
    length_p = 2 * blocks
    total = length_p * length_q
    both = jnp.concatenate([moved_sig, moved_tap], axis=2).transpose(2, 0, 1)
    iota_p = jnp.arange(length_p, dtype=jnp.int32)
    iota_r = jnp.arange(blocks, dtype=jnp.int32)
    iota_q = jnp.arange(length_q, dtype=jnp.int32)
    ang_p = (iota_p[:, None] * iota_r[None, :] % length_p).astype(jnp.float32) * (
        2.0 * math.pi / length_p
    )
    ang_q = (iota_q[:, None] * iota_q[None, :] % length_q).astype(jnp.float32) * (
        2.0 * math.pi / length_q
    )
    ang_t = (iota_p[:, None] * iota_q[None, :] % total).astype(jnp.float32) * (
        2.0 * math.pi / total
    )
    cos_p = jnp.cos(ang_p)
    sin_p = jnp.sin(ang_p)
    cos_q = jnp.cos(ang_q)
    sin_q = jnp.sin(ang_q)
    cos_t = jnp.cos(ang_t)
    sin_t = jnp.sin(ang_t)
    first_re = mixdot("kn,cnq->ckq", cos_p, both)
    first_im = -mixdot("kn,cnq->ckq", sin_p, both)
    tw_re = first_re * cos_t + first_im * sin_t
    tw_im = first_im * cos_t - first_re * sin_t
    spec_re = mixdot("ckq,qm->ckm", tw_re, cos_q) + mixdot("ckq,qm->ckm", tw_im, sin_q)
    spec_im = mixdot("ckq,qm->ckm", tw_im, cos_q) - mixdot("ckq,qm->ckm", tw_re, sin_q)
    half_count = both.shape[0] // 2
    sig_re = spec_re[:half_count]
    sig_im = spec_im[:half_count]
    tap_re = spec_re[half_count:]
    tap_im = spec_im[half_count:]
    prod_re = sig_re * tap_re - sig_im * tap_im
    prod_im = sig_re * tap_im + sig_im * tap_re
    inner_re = mixdot("ckm,mq->ckq", prod_re, cos_q) - mixdot("ckm,mq->ckq", prod_im, sin_q)
    inner_im = mixdot("ckm,mq->ckq", prod_im, cos_q) + mixdot("ckm,mq->ckq", prod_re, sin_q)
    turned_re = inner_re * cos_t - inner_im * sin_t
    turned_im = inner_im * cos_t + inner_re * sin_t
    result = (mixdot("kn,ckq->cnq", cos_p, turned_re) - mixdot("kn,ckq->cnq", sin_p, turned_im)) * (
        1.0 / total
    )
    return lax.all_to_all(
        result.transpose(1, 2, 0).astype(jnp.bfloat16),
        "seq",
        split_axis=1,
        concat_axis=2,
        tiled=True,
    ).astype(jnp.float32)


def body(conv_in, conv_gate, long_filter, skip_gain, queries, keys_in, w_value):
    blocks, slab_rows, channels = conv_in.shape
    my_index = lax.axis_index("seq")
    tokens = blocks * slab_rows
    signal = conv_in.astype(jnp.float32)
    positions = (
        jnp.arange(blocks, dtype=jnp.int32)[:, None] * tokens
        + my_index * slab_rows
        + jnp.arange(slab_rows, dtype=jnp.int32)[None, :]
    )
    convolved = channel_convolve(signal, long_filter)
    mixed = (convolved + skip_gain * signal) * conv_gate.astype(jnp.float32)
    conv_out = mixed.astype(jnp.bfloat16)
    head_size = w_value.shape[1]
    piece = lax.all_gather(conv_out, "chan", axis=2, tiled=True)
    piece_width = piece.shape[2]
    value_sum = jnp.dot(
        piece.reshape(tokens, piece_width), w_value, preferred_element_type=jnp.float32
    )
    values = value_sum.astype(jnp.bfloat16).reshape(blocks, slab_rows, head_size)
    query_rows = queries.reshape(tokens, head_size)
    query_pos = positions.reshape(tokens)
    score_scale = 1.0 / math.sqrt(head_size)
    empty_state = (
        jnp.full((tokens,), -1e30, jnp.float32),
        jnp.zeros((tokens,), jnp.float32),
        jnp.zeros((tokens, head_size), jnp.float32),
    )
    key_piece = lax.all_gather(keys_in, "seq", axis=1, tiled=True)
    value_piece = lax.all_gather(values, "seq", axis=1, tiled=True)
    width_now = key_piece.shape[1]
    target = max(1, 1024 // blocks)
    step_size = 1
    for candidate in range(min(width_now, target), 0, -1):
        step_size = candidate
        break

    def key_step(step_index, current):
        row_best, row_total, row_accum = current
        offset = step_index * step_size
        key_block = lax.dynamic_slice_in_dim(key_piece, offset, step_size, 1).reshape(
            blocks * step_size, head_size
        )
        value_block = lax.dynamic_slice_in_dim(value_piece, offset, step_size, 1).reshape(
            blocks * step_size, head_size
        )
        key_pos = (
            jnp.arange(blocks, dtype=jnp.int32)[:, None] * tokens
            + offset
            + jnp.arange(step_size, dtype=jnp.int32)[None, :]
        ).reshape(blocks * step_size)
        scores = (
            jnp.einsum("qd,kd->qk", query_rows, key_block, preferred_element_type=jnp.float32)
            * score_scale
        )
        allowed = key_pos[None, :] <= query_pos[:, None]
        scores = jnp.where(allowed, scores, -1e30)
        new_best = jnp.maximum(row_best, jnp.max(scores, axis=1))
        factor = jnp.exp(row_best - new_best)
        weights = jnp.where(allowed, jnp.exp(scores - new_best[:, None]), 0.0)
        row_total = row_total * factor + jnp.sum(weights, axis=1)
        row_accum = row_accum * factor[:, None] + jnp.dot(
            weights.astype(jnp.bfloat16), value_block, preferred_element_type=jnp.float32
        )
        return (new_best, row_total, row_accum)

    final_best, final_total, final_accum = lax.fori_loop(
        0, width_now // step_size, key_step, empty_state
    )
    attended = (
        (final_accum / final_total[:, None])
        .astype(jnp.bfloat16)
        .reshape(blocks, slab_rows, head_size)
    )
    return (conv_out, attended)


def solution(mesh):
    return jax.shard_map(
        body,
        mesh=mesh,
        in_specs=(
            P(None, "seq", "chan"),
            P(None, "seq", "chan"),
            P(None, "seq", "chan"),
            P("chan"),
            P(None, "seq", "chan"),
            P(None, "seq", "chan"),
            P(None, "chan"),
        ),
        out_specs=(P(None, "seq", "chan"), P(None, "seq", "chan")),
        check_vma=False,
    )
```

profile of v0, /device:TPU:1, one launch (start us, length us, event | category | flops | bytes accessed | tf_op | source)
XLA Modules:
  0.0 245.0 jit_solution(10891590349229744156)
XLA Ops:
  7.2 0.7 all-gather.3.cloned.1.call-update
  7.9 1.0 convert_element_type.117
  9.2 0.9 reshape.130
  10.0 8.6 %all-to-all-start.1 = ((bf16[32,2,512]{2,1,0:T(2,128)(2,1)}), bf16[32,2,512]{2,1,0:T(2,128)(2,1)S(1)}, u32[]{:S(2)}, u32[]{:S(2)}) async-start(bf16[32,2,512]{2,1,0:T(2,128)(2,1)} %reshape.130), calls=%async_computation.1 | async-start | bytes 131072 | tf_op jit(solution)/shard_map/all_to_all | solution.py:17
  18.6 1.2 copy.75
  19.9 0.9 reshape.132
  20.7 5.2 %all-to-all-done.1 = bf16[32,2,512]{2,1,0:T(2,128)(2,1)S(1)} async-done(((bf16[32,2,512]{2,1,0:T(2,128)(2,1)}), bf16[32,2,512]{2,1,0:T(2,128)(2,1)S(1)}, u32[]{:S(2)}, u32[]{:S(2)}) %all-to-all-start.1) | async-done | bytes 65568 | tf_op jit(solution)/shard_map/all_to_all | solution.py:17
  26.0 3.9 %all-to-all-start = ((bf16[32,2,512]{2,1,0:T(2,128)(2,1)}), bf16[32,2,512]{2,1,0:T(2,128)(2,1)S(1)}, u32[]{:S(2)}, u32[]{:S(2)}) async-start(bf16[32,2,512]{2,1,0:T(2,128)(2,1)} %reshape.132), calls=%async_computation | async-start | bytes 131072 | tf_op jit(solution)/shard_map/all_to_all | solution.py:14
  30.7 6.6 %all-to-all-done = bf16[32,2,512]{2,1,0:T(2,128)(2,1)S(1)} async-done(((bf16[32,2,512]{2,1,0:T(2,128)(2,1)}), bf16[32,2,512]{2,1,0:T(2,128)(2,1)S(1)}, u32[]{:S(2)}, u32[]{:S(2)}) %all-to-all-start) | async-done | bytes 65568 | tf_op jit(solution)/shard_map/all_to_all | solution.py:14
  38.7 5.4 %fusion.30 = f32[4,64,512]{2,1,0:T(8,128)S(1)} fusion(f32[4,64,512]{2,1,0:T(8,128)S(1)} %convolution_bitcast_fusion, f32[4,64,512]{2,1,0:T(8,128)S(1)} %fusion.15, f32[64,512]{1,0:T(8,128)S(1)} %get-tuple-element.210, f32[64,512]{1,0:T(8,128)S(1)} %get-tuple-element.211), kind=kOutput, calls=%fused_computation.51 | convolution fusion | flops 809369600 | bytes 1835008 | tf_op jit(solution)/shard_map/ckq,qm->ckm/dot_general | solution.py:9
  44.1 5.4 %fusion.32 = f32[4,64,512]{2,1,0:T(8,128)S(1)} fusion(f32[4,64,512]{2,1,0:T(8,128)S(1)} %fusion.15, f32[4,64,512]{2,1,0:T(8,128)S(1)} %convolution_bitcast_fusion, f32[64,512]{1,0:T(8,128)S(1)} %get-tuple-element.210, f32[64,512]{1,0:T(8,128)S(1)} %get-tuple-element.211), kind=kOutput, calls=%fused_computation.53 | convolution fusion | flops 809369600 | bytes 1835008 | tf_op jit(solution)/shard_map/ckq,qm->ckm/dot_general | solution.py:9
  49.5 5.4 %convolution_subtract_fusion = f32[4,64,512]{2,1,0:T(8,128)S(1)} fusion(f32[4,64,512]{2,1,0:T(8,128)S(1)} %fusion.30, f32[4,64,512]{2,1,0:T(8,128)S(1)} %fusion.15, f32[4,64,512]{2,1,0:T(8,128)S(1)} %convolution_bitcast_fusion, f32[64,512]{1,0:T(8,128)S(1)} %get-tuple-element.210, f32[64,512]{1,0:T(8,128)S(1)} %get-tuple-element.211), kind=kOutput, calls=%fused_computation.28 | convolution fusion | flops 809500672 | bytes 2359296 | tf_op jit(solution)/shard_map/ckq,qm->ckm/dot_general | solution.py:9
  54.9 5.6 %convolution_add_fusion.1 = f32[4,64,512]{2,1,0:T(8,128)S(1)} fusion(f32[4,64,512]{2,1,0:T(8,128)S(1)} %fusion.32, f32[4,64,512]{2,1,0:T(8,128)S(1)} %convolution_bitcast_fusion, f32[4,64,512]{2,1,0:T(8,128)S(1)} %fusion.15, f32[64,512]{1,0:T(8,128)S(1)} %get-tuple-element.210, f32[64,512]{1,0:T(8,128)S(1)} %get-tuple-element.211), kind=kOutput, calls=%fused_computation.29 | convolution fusion | flops 809500672 | bytes 2359296 | tf_op jit(solution)/shard_map/ckq,qm->ckm/dot_general | solution.py:9
  60.6 4.9 %fusion.28 = f32[2,64,512]{2,1,0:T(8,128)S(1)} fusion(f32[2,64,512]{2,1,0:T(8,128)S(1)} %get-tuple-element.208), kind=kOutput, calls=%fused_computation.49 | convolution fusion | flops 406323200 | bytes 524288 | tf_op jit(solution)/shard_map/ckm,mq->ckq/dot_general | solution.py:9
  65.5 4.9 %fusion.26 = f32[2,64,512]{2,1,0:T(8,128)S(1)} fusion(f32[2,64,512]{2,1,0:T(8,128)S(1)} %get-tuple-element.209), kind=kOutput, calls=%fused_computation.47 | convolution fusion | flops 406323200 | bytes 524288 | tf_op jit(solution)/shard_map/ckm,mq->ckq/dot_general | solution.py:9
  70.4 4.9 %convolution_subtract_fusion.1 = f32[2,64,512]{2,1,0:T(8,128)S(1)} fusion(f32[2,64,512]{2,1,0:T(8,128)S(1)} %fusion.28, f32[2,64,512]{2,1,0:T(8,128)S(1)} %get-tuple-element.209), kind=kOutput, calls=%fused_computation.34 | convolution fusion | flops 406388736 | bytes 786432 | tf_op jit(solution)/shard_map/ckm,mq->ckq/dot_general | solution.py:9
  75.2 5.1 %convolution_add_fusion.2 = f32[2,64,512]{2,1,0:T(8,128)S(1)} fusion(f32[2,64,512]{2,1,0:T(8,128)S(1)} %fusion.26, f32[2,64,512]{2,1,0:T(8,128)S(1)} %get-tuple-element.208), kind=kOutput, calls=%fused_computation.33 | convolution fusion | flops 406388736 | bytes 786432 | tf_op jit(solution)/shard_map/ckm,mq->ckq/dot_general | solution.py:9
  81.4 0.9 reshape.134
  82.2 3.9 %all-to-all-start.2 = ((bf16[32,2,512]{2,1,0:T(2,128)(2,1)}), bf16[32,2,512]{2,1,0:T(2,128)(2,1)S(1)}, u32[]{:S(2)}, u32[]{:S(2)}) async-start(bf16[32,2,512]{2,1,0:T(2,128)(2,1)} %reshape.134), calls=%async_computation.2 | async-start | bytes 131072 | tf_op jit(solution)/shard_map/all_to_all | solution.py:64
  86.5 7.1 %all-to-all-done.2 = bf16[32,2,512]{2,1,0:T(2,128)(2,1)S(1)} async-done(((bf16[32,2,512]{2,1,0:T(2,128)(2,1)}), bf16[32,2,512]{2,1,0:T(2,128)(2,1)S(1)}, u32[]{:S(2)}, u32[]{:S(2)}) %all-to-all-start.2) | async-done | bytes 65568 | tf_op jit(solution)/shard_map/all_to_all | solution.py:64
  94.1 28.8 %all_gather.10 = bf16[32,16,512]{0,1,2:T(8,128)(2,1)S(1)} all-gather(bf16[32,16,64]{0,1,2:T(8,128)(2,1)S(1)} %fusion.38), channel_id=1, replica_groups=mesh['seq'=32,'chan'=8] {'chan'}, dimensions={2}, use_global_device_ids=true | all-gather | bytes 589824 | tf_op jit(solution)/shard_map/all_gather | solution.py:87
  123.0 2.2 copy.86
  125.2 1.0 convolution_convert_fusion
  126.2 1.0 copy.87
  127.2 53.7 %all-gather.5.cloned.1.call-done = bf16[32,512,128]{2,1,0:T(8,128)(2,1)} async-done(((bf16[32,16,128]{2,1,0:T(8,128)(2,1)}), bf16[32,512,128]{2,1,0:T(8,128)(2,1)}) %all-gather.5.cloned.1.call-update) | async-done | bytes 4194320 | tf_op jit(solution)/shard_map/all_gather | solution.py:102
  180.8 56.5 %while.18 = (s32[]{:T(128)}, f32[512]{0:T(512)S(1)}, f32[512]{0:T(512)S(1)}, f32[512,128]{1,0:T(8,128)S(1)}, bf16[32,512,128]{2,1,0:T(8,128)(2,1)}, /*index=5*/b...) while((s32[]{:T(128)}, f32[512]{0:T(512)S(1)}, ...), condition=%wide.region_3.4_spmd.clone, body=%wide.region_0.3_spmd.clone.sunk | while | flops 277024832 | bytes 8589887 | solution.py:139
  181.1 1.1 constant_dynamic-slice_fusion.3
  183.3 1.0 convolution_add_fusion.4
  184.7 1.1 constant_dynamic-slice_fusion.3
  186.2 0.6 fusion.155
  186.9 1.0 convolution_add_fusion.4
  188.2 1.1 constant_dynamic-slice_fusion.3
  189.7 0.6 fusion.155
  190.4 1.0 convolution_add_fusion.4
  191.7 1.1 constant_dynamic-slice_fusion.3
  193.3 0.6 fusion.155
  193.9 1.0 convolution_add_fusion.4
  195.3 1.1 constant_dynamic-slice_fusion.3
  196.8 0.6 fusion.155
  197.5 1.0 convolution_add_fusion.4
  198.8 1.1 constant_dynamic-slice_fusion.3
  200.3 0.6 fusion.155
  201.0 1.0 convolution_add_fusion.4
  202.3 1.1 constant_dynamic-slice_fusion.3
  204.5 1.0 convolution_add_fusion.4
  205.9 1.1 constant_dynamic-slice_fusion.3
  208.1 1.0 convolution_add_fusion.4
  209.4 1.1 constant_dynamic-slice_fusion.3
  211.6 1.0 convolution_add_fusion.4
  212.9 1.1 constant_dynamic-slice_fusion.3
  215.1 1.0 convolution_add_fusion.4
  216.4 1.1 constant_dynamic-slice_fusion.3
  218.7 1.0 convolution_add_fusion.4
  220.0 1.1 constant_dynamic-slice_fusion.3
  222.2 1.0 convolution_add_fusion.4
  223.5 1.1 constant_dynamic-slice_fusion.3
  225.7 1.0 convolution_add_fusion.4
  227.0 1.1 constant_dynamic-slice_fusion.3
  229.2 1.0 convolution_add_fusion.4
  230.6 1.1 constant_dynamic-slice_fusion.3
  232.8 1.0 convolution_add_fusion.4
  234.1 1.1 constant_dynamic-slice_fusion.3
  236.3 1.0 convolution_add_fusion.4
  237.3 0.8 divide_convert_fusion
  (191 shorter events, 24.0 us)
Async XLA Ops:
  7.2 118.0 %copy-start = (bf16[512,128]{1,0:T(8,128)(2,1)S(1)}, bf16[512,128]{1,0:T(8,128)(2,1)}, u32[]{:S(2)}) copy-start(bf16[512,128]{1,0:T(8,128)(2,1)} %param.15) | copy-start | bytes 393220
  7.2 120.0 %all-gather.3.cloned.1.call-start = ((), (), s32[]{:S(2)}) async-start(), calls=%async_computation.3 | async-start | bytes 4325376 | tf_op jit(solution)/shard_map/all_gather | solution.py:101
  10.0 15.9 %all-to-all-start.1 = ((bf16[32,2,512]{2,1,0:T(2,128)(2,1)}), bf16[32,2,512]{2,1,0:T(2,128)(2,1)S(1)}, u32[]{:S(2)}, u32[]{:S(2)}) async-start(bf16[32,2,512]{2,1,0:T(2,128)(2,1)} %reshape.130), calls=%async_computation.1 | async-start | bytes 131072 | tf_op jit(solution)/shard_map/all_to_all | solution.py:17
  26.0 11.3 %all-to-all-start = ((bf16[32,2,512]{2,1,0:T(2,128)(2,1)}), bf16[32,2,512]{2,1,0:T(2,128)(2,1)S(1)}, u32[]{:S(2)}, u32[]{:S(2)}) async-start(bf16[32,2,512]{2,1,0:T(2,128)(2,1)} %reshape.132), calls=%async_computation | async-start | bytes 131072 | tf_op jit(solution)/shard_map/all_to_all | solution.py:14
  80.3 5.9 %copy-start.1 = (bf16[32,16,64]{2,1,0:T(8,128)(2,1)S(1)}, bf16[32,16,64]{2,1,0:T(8,128)(2,1)}, u32[]{:S(2)}) copy-start(bf16[32,16,64]{2,1,0:T(8,128)(2,1)} %param.10) | copy-start | bytes 196612
  81.2 12.8 %copy-start.2 = (f32[64]{0:T(128)S(1)}, f32[64]{0:T(128)}, u32[]{:S(2)}) copy-start(f32[64]{0:T(128)} %param.12) | copy-start | bytes 772
  82.2 11.4 %all-to-all-start.2 = ((bf16[32,2,512]{2,1,0:T(2,128)(2,1)}), bf16[32,2,512]{2,1,0:T(2,128)(2,1)S(1)}, u32[]{:S(2)}, u32[]{:S(2)}) async-start(bf16[32,2,512]{2,1,0:T(2,128)(2,1)} %reshape.134), calls=%async_computation.2 | async-start | bytes 131072 | tf_op jit(solution)/shard_map/all_to_all | solution.py:64
  86.2 94.6 %all-gather.5.cloned.1.call-start = ((), (), s32[]{:S(2)}) async-start(), calls=%async_computation.4 | async-start | bytes 4325376 | tf_op jit(solution)/shard_map/all_gather | solution.py:102
  123.0 57.8 %copy-start.3 = (bf16[32,16,128]{2,1,0:T(8,128)(2,1)S(1)}, bf16[32,16,128]{2,1,0:T(8,128)(2,1)}, u32[]{:S(2)}) copy-start(bf16[32,16,128]{2,1,0:T(8,128)(2,1)} %param.13) | copy-start | bytes 393220
Sparse Core Ops, SparseCore 0:
  10.5 58.7 all-gather.2
  126.3 54.5 all-gather.4
where the time goes:
time: 246 us; the launch traced here: 245 us
  waiting for transfers between devices  73.2 us (30%)
  matrix products  67.3 us (27%)
  blocking collectives  28.8 us (12%)
  local copies, waits for them, and re-layouts  28.4 us (12%)
  starting transfers between devices  16.5 us (7%)
  other arithmetic  15.3 us (6%)
  between operations  14.4 us (6%)
    all_gather x1, waiting for transfers between devices, body(): value_piece = lax.all_gather(values, 'seq', axis=1, tiled=True)  53.7 us
    dot_general x12, matrix products, mixdot(): return jnp.einsum(form, left, right, precision=lax.Precision.HIGHEST)  43.3 us
    all_gather x1, blocking collectives, body(): piece = lax.all_gather(conv_out, 'chan', axis=2, tiled=True)  28.8 us
    dynamic_slice x16, local copies, waits for them, and re-layouts, key_step(): lax.dynamic_slice_in_dim(value_piece, offset, step_size, 1)  17.2 us
    dot_general x16, matrix products, key_step(): jnp.dot(weights.astype(jnp.bfloat16), value_block, preferred_element_type...  15.7 us
    reduce_sum x16, other arithmetic, key_step(): row_total = row_total * factor + jnp.sum(weights, axis=1)  9.97 us
    all_to_all x1, starting transfers between devices, channel_convolve(): lax.all_to_all(long_filter.astype(jnp.bfloat16), 'seq', split_axis=2, con...  8.59 us
    dot_general x16, matrix products, key_step(): jnp.einsum('qd,kd->qk', query_rows, key_block, preferred_element_type=jnp...  7.38 us
  transfers between devices with their start and end apart: 5, of which 4 were waited for; matrix products, arithmetic and copies ran while one was open for 22% of the time, Pallas kernels for 0%

commit v1 on v0

--- a/solution.py
+++ b/solution.py
@@ -3,6 +3,7 @@
 import jax.numpy as jnp
 from jax import lax
 from jax.sharding import PartitionSpec as P
+from jax.lax import all_to_all, axis_size
 
 
 def mixdot(form, left, right):
@@ -99,7 +100,9 @@
         jnp.zeros((tokens, head_size), jnp.float32),
     )
     key_piece = lax.all_gather(keys_in, "seq", axis=1, tiled=True)
-    value_piece = lax.all_gather(values, "seq", axis=1, tiled=True)
+    shaped = axis_size("seq")
+    low = jnp.concatenate(shaped * [values], axis=1)
+    value_piece = all_to_all(low, "seq", 1, 1, tiled=True)
     width_now = key_piece.shape[1]
     target = max(1, 1024 // blocks)
     step_size = 1

time: 246 us -> 290 us (1.18)
  local copies, waits for them, and re-layouts: 28.4 us -> 66.1 us
  starting transfers between devices: 16.5 us -> 25.8 us
  waiting for transfers between devices: 73.2 us -> 68.2 us
    all_gather x1 -> x0, waiting for transfers between devices: 53.7 us -> none  [body(): value_piece = lax.all_gather(values, 'seq', axis=1, tiled=True)]
    all_to_all x0 -> x1, waiting for transfers between devices: none -> 49.4 us  [body(): value_piece = all_to_all(low, 'seq', 1, 1, tiled=True)]
    unnamed x17 -> x48, local copies, waits for them, and re-layouts: 5.61 us -> 27 us
    dynamic_slice x0 -> x16, local copies, waits for them, and re-layouts: none -> 15.7 us  [key_step(): lax.dynamic_slice_in_dim(key_piece, offset, step_size, 1)]
    all_to_all x0 -> x1, starting transfers between devices: none -> 9.33 us  [body(): value_piece = all_to_all(low, 'seq', 1, 1, tiled=True)]
    all_to_all x1, starting transfers between devices: 3.9 us -> 8.59 us  [channel_convolve(): lax.all_to_all(signal.astype(jnp.bfloat16), 'seq', split_axis=2, concat_a...]
    all_to_all x1, starting transfers between devices: 8.59 us -> 3.9 us  [channel_convolve(): lax.all_to_all(long_filter.astype(jnp.bfloat16), 'seq', split_axis=2, con...]
    dynamic_slice x16 -> x32, local copies, waits for them, and re-layouts: 17.2 us -> 17.3 us  [key_step(): lax.dynamic_slice_in_dim(value_piece, offset, step_size, 1)]
  transfers between devices with their start and end apart: 5 -> 5, of which waited for: 4 -> 4; matrix products, arithmetic and copies ran while one was open for 22% -> 10% of each run, Pallas kernels for 0% -> 0%
where the time goes in v1:
time: 290 us; the launch traced here: 287 us
  waiting for transfers between devices  68.2 us (24%)
  matrix products  66.7 us (23%)
  local copies, waits for them, and re-layouts  66.1 us (23%)
  blocking collectives  29.2 us (10%)
  starting transfers between devices  25.8 us (9%)
  other arithmetic  15.3 us (5%)
  between operations  14.4 us (5%)
    all_to_all x1, waiting for transfers between devices, body(): value_piece = all_to_all(low, 'seq', 1, 1, tiled=True)  49.4 us
    dot_general x12, matrix products, mixdot(): return jnp.einsum(form, left, right, precision=lax.Precision.HIGHEST)  43.3 us
    all_gather x1, blocking collectives, body(): piece = lax.all_gather(conv_out, 'chan', axis=2, tiled=True)  29.2 us
    unnamed x48, local copies, waits for them, and re-layouts  27 us
    dynamic_slice x32, local copies, waits for them, and re-layouts, key_step(): lax.dynamic_slice_in_dim(value_piece, offset, step_size, 1)  17.3 us
    dynamic_slice x16, local copies, waits for them, and re-layouts, key_step(): lax.dynamic_slice_in_dim(key_piece, offset, step_size, 1)  15.7 us
    dot_general x16, matrix products, key_step(): jnp.dot(weights.astype(jnp.bfloat16), value_block, preferred_element_type...  15.6 us
    reduce_sum x16, other arithmetic, key_step(): row_total = row_total * factor + jnp.sum(weights, axis=1)  9.95 us
  transfers between devices with their start and end apart: 5, of which 4 were waited for; matrix products, arithmetic and copies ran while one was open for 10% of the time, Pallas kernels for 0%

profile of v1, /device:TPU:1, one launch (start us, length us, event | category | flops | bytes accessed | tf_op | source)
XLA Modules:
  0.0 286.9 jit_solution(2714387805621647393)
XLA Ops:
  7.2 1.2 copy.174
  9.3 8.6 %all-to-all-start = ((bf16[32,2,512]{2,1,0:T(2,128)(2,1)}), bf16[32,2,512]{2,1,0:T(2,128)(2,1)S(1)}, u32[]{:S(2)}, u32[]{:S(2)}) async-start(bf16[32,2,512]{2,1,0:T(2,128)(2,1)} %reshape.132), calls=%async_computation | async-start | bytes 131072 | tf_op jit(solution)/shard_map/all_to_all | solution.py:15
  20.0 5.2 %all-to-all-done = bf16[32,2,512]{2,1,0:T(2,128)(2,1)S(1)} async-done(((bf16[32,2,512]{2,1,0:T(2,128)(2,1)}), bf16[32,2,512]{2,1,0:T(2,128)(2,1)S(1)}, u32[]{:S(2)}, u32[]{:S(2)}) %all-to-all-start) | async-done | bytes 65568 | tf_op jit(solution)/shard_map/all_to_all | solution.py:15
  25.2 3.9 %all-to-all-start.1 = ((bf16[32,2,512]{2,1,0:T(2,128)(2,1)}), bf16[32,2,512]{2,1,0:T(2,128)(2,1)S(1)}, u32[]{:S(2)}, u32[]{:S(2)}) async-start(bf16[32,2,512]{2,1,0:T(2,128)(2,1)} %reshape.130), calls=%async_computation.1 | async-start | bytes 131072 | tf_op jit(solution)/shard_map/all_to_all | solution.py:18
  30.0 6.6 %all-to-all-done.1 = bf16[32,2,512]{2,1,0:T(2,128)(2,1)S(1)} async-done(((bf16[32,2,512]{2,1,0:T(2,128)(2,1)}), bf16[32,2,512]{2,1,0:T(2,128)(2,1)S(1)}, u32[]{:S(2)}, u32[]{:S(2)}) %all-to-all-start.1) | async-done | bytes 65568 | tf_op jit(solution)/shard_map/all_to_all | solution.py:18
  37.9 5.4 %fusion.32 = f32[4,64,512]{2,1,0:T(8,128)S(1)} fusion(f32[4,64,512]{2,1,0:T(8,128)S(1)} %fusion.15, f32[4,64,512]{2,1,0:T(8,128)S(1)} %convolution_bitcast_fusion, f32[64,512]{1,0:T(8,128)S(1)} %get-tuple-element.240, f32[64,512]{1,0:T(8,128)S(1)} %get-tuple-element.241), kind=kOutput, calls=%fused_computation.53 | convolution fusion | flops 809369600 | bytes 1835008 | tf_op jit(solution)/shard_map/ckq,qm->ckm/dot_general | solution.py:10
  43.3 5.4 %fusion.30 = f32[4,64,512]{2,1,0:T(8,128)S(1)} fusion(f32[4,64,512]{2,1,0:T(8,128)S(1)} %convolution_bitcast_fusion, f32[4,64,512]{2,1,0:T(8,128)S(1)} %fusion.15, f32[64,512]{1,0:T(8,128)S(1)} %get-tuple-element.240, f32[64,512]{1,0:T(8,128)S(1)} %get-tuple-element.241), kind=kOutput, calls=%fused_computation.51 | convolution fusion | flops 809369600 | bytes 1835008 | tf_op jit(solution)/shard_map/ckq,qm->ckm/dot_general | solution.py:10
  48.8 5.4 %convolution_add_fusion.1 = f32[4,64,512]{2,1,0:T(8,128)S(1)} fusion(f32[4,64,512]{2,1,0:T(8,128)S(1)} %fusion.32, f32[4,64,512]{2,1,0:T(8,128)S(1)} %convolution_bitcast_fusion, f32[4,64,512]{2,1,0:T(8,128)S(1)} %fusion.15, f32[64,512]{1,0:T(8,128)S(1)} %get-tuple-element.240, f32[64,512]{1,0:T(8,128)S(1)} %get-tuple-element.241), kind=kOutput, calls=%fused_computation.29 | convolution fusion | flops 809500672 | bytes 2359296 | tf_op jit(solution)/shard_map/ckq,qm->ckm/dot_general | solution.py:10
  54.2 5.6 %convolution_subtract_fusion = f32[4,64,512]{2,1,0:T(8,128)S(1)} fusion(f32[4,64,512]{2,1,0:T(8,128)S(1)} %fusion.30, f32[4,64,512]{2,1,0:T(8,128)S(1)} %fusion.15, f32[4,64,512]{2,1,0:T(8,128)S(1)} %convolution_bitcast_fusion, f32[64,512]{1,0:T(8,128)S(1)} %get-tuple-element.240, f32[64,512]{1,0:T(8,128)S(1)} %get-tuple-element.241), kind=kOutput, calls=%fused_computation.28 | convolution fusion | flops 809500672 | bytes 2359296 | tf_op jit(solution)/shard_map/ckq,qm->ckm/dot_general | solution.py:10
  59.9 4.9 %fusion.28 = f32[2,64,512]{2,1,0:T(8,128)S(1)} fusion(f32[2,64,512]{2,1,0:T(8,128)S(1)} %get-tuple-element.238), kind=kOutput, calls=%fused_computation.49 | convolution fusion | flops 406323200 | bytes 524288 | tf_op jit(solution)/shard_map/ckm,mq->ckq/dot_general | solution.py:10
  64.8 4.9 %fusion.26 = f32[2,64,512]{2,1,0:T(8,128)S(1)} fusion(f32[2,64,512]{2,1,0:T(8,128)S(1)} %get-tuple-element.239), kind=kOutput, calls=%fused_computation.47 | convolution fusion | flops 406323200 | bytes 524288 | tf_op jit(solution)/shard_map/ckm,mq->ckq/dot_general | solution.py:10
  69.6 4.9 %convolution_subtract_fusion.1 = f32[2,64,512]{2,1,0:T(8,128)S(1)} fusion(f32[2,64,512]{2,1,0:T(8,128)S(1)} %fusion.28, f32[2,64,512]{2,1,0:T(8,128)S(1)} %get-tuple-element.239), kind=kOutput, calls=%fused_computation.34 | convolution fusion | flops 406388736 | bytes 786432 | tf_op jit(solution)/shard_map/ckm,mq->ckq/dot_general | solution.py:10
  74.5 5.1 %convolution_add_fusion.2 = f32[2,64,512]{2,1,0:T(8,128)S(1)} fusion(f32[2,64,512]{2,1,0:T(8,128)S(1)} %fusion.26, f32[2,64,512]{2,1,0:T(8,128)S(1)} %get-tuple-element.238), kind=kOutput, calls=%fused_computation.33 | convolution fusion | flops 406388736 | bytes 786432 | tf_op jit(solution)/shard_map/ckm,mq->ckq/dot_general | solution.py:10
  81.5 3.9 %all-to-all-start.2 = ((bf16[32,2,512]{2,1,0:T(2,128)(2,1)}), bf16[32,2,512]{2,1,0:T(2,128)(2,1)S(1)}, u32[]{:S(2)}, u32[]{:S(2)}) async-start(bf16[32,2,512]{2,1,0:T(2,128)(2,1)} %reshape.134), calls=%async_computation.2 | async-start | bytes 131072 | tf_op jit(solution)/shard_map/all_to_all | solution.py:65
  86.4 6.4 %all-to-all-done.2 = bf16[32,2,512]{2,1,0:T(2,128)(2,1)S(1)} async-done(((bf16[32,2,512]{2,1,0:T(2,128)(2,1)}), bf16[32,2,512]{2,1,0:T(2,128)(2,1)S(1)}, u32[]{:S(2)}, u32[]{:S(2)}) %all-to-all-start.2) | async-done | bytes 65568 | tf_op jit(solution)/shard_map/all_to_all | solution.py:65
  93.4 29.2 %all_gather.7 = bf16[32,16,512]{0,1,2:T(8,128)(2,1)S(1)} all-gather(bf16[32,16,64]{0,1,2:T(8,128)(2,1)S(1)} %fusion.38), channel_id=1, replica_groups=mesh['seq'=32,'chan'=8] {'chan'}, dimensions={2}, use_global_device_ids=true | all-gather | bytes 589824 | tf_op jit(solution)/shard_map/all_gather | solution.py:88
  122.6 2.2 copy.185
  147.1 9.3 %all-to-all-start.3 = ((bf16[32,512,128]{2,0,1:T(8,128)(2,1)}), bf16[32,512,128]{2,0,1:T(8,128)(2,1)}, u32[]{:S(2)}, u32[]{:S(2)}) async-start(bf16[32,512,128]{2,0,1:T(8,128)(2,1)} %constant_dynamic-update-slice_fusion), calls=%async_computation.3 | async-start | bytes 8388608 | tf_op jit(solution)/shard_map/all_to_all | solution.py:105
  157.5 49.4 %all-to-all-done.3 = bf16[32,512,128]{2,0,1:T(8,128)(2,1)} async-done(((bf16[32,512,128]{2,0,1:T(8,128)(2,1)}), bf16[32,512,128]{2,0,1:T(8,128)(2,1)}, u32[]{:S(2)}, u32[]{:S(2)}) %all-to-all-start.3) | async-done | bytes 4194336 | tf_op jit(solution)/shard_map/all_to_all | solution.py:105
  206.9 72.4 %while.18 = (s32[]{:T(128)}, f32[512]{0:T(512)S(1)}, f32[512]{0:T(512)S(1)}, f32[512,128]{1,0:T(8,128)S(1)}, bf16[32,512,128]{2,1,0:T(8,128)(2,1)}, /*index=5*/b...) while((s32[]{:T(128)}, f32[512]{0:T(512)S(1)}, ...), condition=%wide.region_3.4_spmd.clone, body=%wide.region_0.3_spmd.clone.sunk | while | flops 277024832 | bytes 9114171 | solution.py:142
  209.3 1.0 constant_dynamic-slice_fusion.5
  210.4 1.0 convolution_add_fusion.4
  211.4 1.0 constant_dynamic-slice_fusion.4
  213.8 1.0 constant_dynamic-slice_fusion.5
  214.9 1.0 convolution_add_fusion.4
  215.9 1.0 constant_dynamic-slice_fusion.4
  218.3 1.0 constant_dynamic-slice_fusion.5
  219.4 1.0 convolution_add_fusion.4
  220.4 1.0 constant_dynamic-slice_fusion.4
  222.9 1.0 constant_dynamic-slice_fusion.5
  223.9 1.0 convolution_add_fusion.4
  225.0 1.0 constant_dynamic-slice_fusion.4
  227.4 1.0 constant_dynamic-slice_fusion.5
  228.5 1.0 convolution_add_fusion.4
  229.5 1.0 constant_dynamic-slice_fusion.4
  231.9 1.0 constant_dynamic-slice_fusion.5
  233.0 1.0 convolution_add_fusion.4
  234.0 1.0 constant_dynamic-slice_fusion.4
  236.4 1.0 constant_dynamic-slice_fusion.5
  237.5 1.0 convolution_add_fusion.4
  238.5 1.0 constant_dynamic-slice_fusion.4
  241.0 1.0 constant_dynamic-slice_fusion.5
  242.1 1.0 convolution_add_fusion.4
  243.1 1.0 constant_dynamic-slice_fusion.4
  245.5 1.0 constant_dynamic-slice_fusion.5
  246.6 1.0 convolution_add_fusion.4
  247.6 1.0 constant_dynamic-slice_fusion.4
  250.0 1.0 constant_dynamic-slice_fusion.5
  251.1 1.0 convolution_add_fusion.4
  252.1 1.0 constant_dynamic-slice_fusion.4
  254.6 1.0 constant_dynamic-slice_fusion.5
  255.7 1.0 convolution_add_fusion.4
  256.7 1.0 constant_dynamic-slice_fusion.4
  259.1 1.0 constant_dynamic-slice_fusion.5
  261.2 1.0 constant_dynamic-slice_fusion.4
  264.7 1.0 convolution_add_fusion.4
  265.7 1.0 constant_dynamic-slice_fusion.4
  268.1 1.0 constant_dynamic-slice_fusion.5
  269.2 1.0 convolution_add_fusion.4
  270.3 1.0 constant_dynamic-slice_fusion.4
  272.7 1.0 constant_dynamic-slice_fusion.5
  273.8 1.0 convolution_add_fusion.4
  274.8 1.0 constant_dynamic-slice_fusion.4
  277.2 1.0 constant_dynamic-slice_fusion.5
  (254 shorter events, 61.0 us)
Async XLA Ops:
  7.2 117.6 %copy-start = (bf16[512,128]{1,0:T(8,128)(2,1)S(1)}, bf16[512,128]{1,0:T(8,128)(2,1)}, u32[]{:S(2)}) copy-start(bf16[512,128]{1,0:T(8,128)(2,1)} %param.15) | copy-start | bytes 393220
  9.3 15.9 %all-to-all-start = ((bf16[32,2,512]{2,1,0:T(2,128)(2,1)}), bf16[32,2,512]{2,1,0:T(2,128)(2,1)S(1)}, u32[]{:S(2)}, u32[]{:S(2)}) async-start(bf16[32,2,512]{2,1,0:T(2,128)(2,1)} %reshape.132), calls=%async_computation | async-start | bytes 131072 | tf_op jit(solution)/shard_map/all_to_all | solution.py:15
  25.2 11.3 %all-to-all-start.1 = ((bf16[32,2,512]{2,1,0:T(2,128)(2,1)}), bf16[32,2,512]{2,1,0:T(2,128)(2,1)S(1)}, u32[]{:S(2)}, u32[]{:S(2)}) async-start(bf16[32,2,512]{2,1,0:T(2,128)(2,1)} %reshape.130), calls=%async_computation.1 | async-start | bytes 131072 | tf_op jit(solution)/shard_map/all_to_all | solution.py:18
  74.5 11.6 %copy-start.1 = (bf16[32,16,64]{2,1,0:T(8,128)(2,1)S(1)}, bf16[32,16,64]{2,1,0:T(8,128)(2,1)}, u32[]{:S(2)}) copy-start(bf16[32,16,64]{2,1,0:T(8,128)(2,1)} %param.10) | copy-start | bytes 196612
  74.5 18.7 %copy-start.2 = (f32[64]{0:T(128)S(1)}, f32[64]{0:T(128)}, u32[]{:S(2)}) copy-start(f32[64]{0:T(128)} %param.12) | copy-start | bytes 772
  81.5 11.3 %all-to-all-start.2 = ((bf16[32,2,512]{2,1,0:T(2,128)(2,1)}), bf16[32,2,512]{2,1,0:T(2,128)(2,1)S(1)}, u32[]{:S(2)}, u32[]{:S(2)}) async-start(bf16[32,2,512]{2,1,0:T(2,128)(2,1)} %reshape.134), calls=%async_computation.2 | async-start | bytes 131072 | tf_op jit(solution)/shard_map/all_to_all | solution.py:65
  85.4 121.4 %all-gather.2.cloned.1.call-start = ((), (), s32[]{:S(2)}) async-start(), calls=%async_computation.4 | async-start | bytes 4325376 | tf_op jit(solution)/shard_map/all_gather | solution.py:102
  147.1 59.7 %copy-start.3 = (bf16[32,16,128]{2,1,0:T(8,128)(2,1)S(1)}, bf16[32,16,128]{2,1,0:T(8,128)(2,1)}, u32[]{:S(2)}) copy-start(bf16[32,16,128]{2,1,0:T(8,128)(2,1)} %param.13) | copy-start | bytes 393220
  147.1 59.7 %all-to-all-start.3 = ((bf16[32,512,128]{2,0,1:T(8,128)(2,1)}), bf16[32,512,128]{2,0,1:T(8,128)(2,1)}, u32[]{:S(2)}, u32[]{:S(2)}) async-start(bf16[32,512,128]{2,0,1:T(8,128)(2,1)} %constant_dynamic-update-slice_fusion), calls=%async_computation.3 | async-start | bytes 8388608 | tf_op jit(solution)/shard_map/all_to_all | solution.py:105
Sparse Core Ops, SparseCore 0:
  88.7 57.3 all-gather.1
